TPU v7x, 32 devices: a whole 2x2x4 slice. The times are simulated.
32 devices in a mesh: seq: 8 (over y, x, core), mlp: 4 (over z).
Axes of the slice: x: 2, y: 2, z: 4, core: 2. Of those that a mesh axis runs over, the one named last changes fastest.
Arguments:
- hidden_in: bfloat16 [36864, 768], P(('seq', 'mlp')), may hold values from -6 to 6
- cotangent: bfloat16 [36864, 768], P(('seq', 'mlp')), may hold values from -6 to 6
- w_qkv: bfloat16 [768, 2304], P(None, ('seq', 'mlp')), may hold values from -0.21875 to 0.21875
- w_attn_out: bfloat16 [768, 768], P(None, ('seq', 'mlp')), may hold values from -2.5 to 2.5
- attn_gain: bfloat16 [768], P(('seq', 'mlp')), may hold values from 0.099609375 to 1.8984375
- mlp_gain: bfloat16 [768], P(('seq', 'mlp')), may hold values from 0.099609375 to 1.8984375
- w_gate: bfloat16 [768, 1152], P(None, 'mlp'), may hold values from -0.21875 to 0.21875
- w_up: bfloat16 [768, 1152], P(None, 'mlp'), may hold values from -0.21875 to 0.21875
- w_down: bfloat16 [1152, 768], P('mlp'), may hold values from -0.1875 to 0.1875
- doc_lengths: int32 [32, 5], P(('seq', 'mlp')), may hold values from 1 to 1024, 1152 in all within a row
Outputs:
- layer_out: bfloat16 [36864, 768], P(('seq', 'mlp'))
- grad_hidden: bfloat16 [36864, 768], P(('seq', 'mlp'))
- grad_qkv: float32 [768, 2304], P(None, ('seq', 'mlp'))
- grad_attn_out: float32 [768, 768], P(None, ('seq', 'mlp'))
- grad_attn_gain: float32 [768], P(('seq', 'mlp'))
- grad_mlp_gain: float32 [768], P(('seq', 'mlp'))
- grad_gate: float32 [768, 1152], P(None, 'mlp')
- grad_up: float32 [768, 1152], P(None, 'mlp')
- grad_down: float32 [1152, 768], P('mlp')
Inputs may be any that keep to these rules, and one draw needn't show every extreme that they name: `doc_lengths`: row b gives the lengths of the 4 documents packed in order from the start of block b, then the number of padding rows at its end; a row sums to 1152.
All inputs are finite; a program needn't handle non-finite values.
Results may differ from a plain program's by a relative error of at most 0.015.
Values may be sent and summed in bfloat16 or wider, within the bound.
No kernel may reach another device: no remote copies, remote signals or barrier semaphores. Data moves between devices by JAX's collectives and lax.ppermute only.
A program may use at most 192 MiB of HBM per device.

v0:
```python
import math

import jax
import jax.numpy as jnp
from jax import lax
from jax.sharding import PartitionSpec as P

HEADS = 12
HEAD_DIM = 64


eps_norm = 1e-05
theta_rope = 160000.0
contract_rows = (((0,), (0,)), ((), ()))
contract_cols = (((1,), (1,)), ((), ()))


def layout(doc_lengths, row_count):
    lengths = doc_lengths[0]
    slot_count = lengths.shape[0]
    doc_ends = jnp.cumsum(lengths)
    starts = doc_ends - lengths
    places = jnp.arange(row_count, dtype=jnp.int32)
    doc_ids = jnp.sum((places[:, None] >= doc_ends[None, :]).astype(jnp.int32), axis=1)
    picked = doc_ids[:, None] == jnp.arange(slot_count, dtype=jnp.int32)[None, :]
    offsets = jnp.sum(jnp.where(picked, starts[None, :], 0), axis=1)
    return (doc_ids, places - offsets, doc_ids < slot_count - 1)


def rope_tables(positions):
    half_dim = HEAD_DIM // 2
    frequency = jnp.exp(
        jnp.arange(half_dim, dtype=jnp.float32) * (-2.0 * math.log(theta_rope) / HEAD_DIM)
    )
    angles = positions.astype(jnp.float32)[..., None] * frequency
    cos_table = jnp.concatenate([jnp.cos(angles), jnp.cos(angles)], axis=-1)
    sin_table = jnp.concatenate([jnp.sin(angles), jnp.sin(angles)], axis=-1)
    return (cos_table, sin_table)


def rotate_half(vector):
    half_dim = vector.shape[-1] // 2
    return jnp.concatenate([-vector[..., half_dim:], vector[..., :half_dim]], axis=-1)


def rotate_back(vector):
    half_dim = vector.shape[-1] // 2
    return jnp.concatenate([vector[..., half_dim:], -vector[..., :half_dim]], axis=-1)


def standardize(value):
    mean_value = jnp.mean(value, axis=-1, keepdims=True)
    centered = value - mean_value
    inverse = lax.rsqrt(jnp.mean(centered * centered, axis=-1, keepdims=True) + eps_norm)
    return (centered * inverse, inverse)


def norm_back(grad_normed, normed, inverse, gain):
    scaled = grad_normed * gain
    return inverse * (
        scaled
        - jnp.mean(scaled, axis=-1, keepdims=True)
        - normed * jnp.mean(scaled * normed, axis=-1, keepdims=True)
    )


def gelu_exact(value):
    return 0.5 * value * (1.0 + lax.erf(value * (1.0 / math.sqrt(2.0))))


def geglu_back(grad_inner, gate_pre, up_pre):
    cumulative = 0.5 * (1.0 + lax.erf(gate_pre * (1.0 / math.sqrt(2.0))))
    density = jnp.exp(-0.5 * gate_pre * gate_pre) * (1.0 / math.sqrt(2.0 * math.pi))
    slope = cumulative + gate_pre * density
    grad_gate = (grad_inner * up_pre * slope).astype(jnp.bfloat16)
    grad_up = (grad_inner * (gate_pre * cumulative)).astype(jnp.bfloat16)
    return (grad_gate, grad_up)


def shards(
    hidden_in, cotangent, w_qkv, w_attn_out, attn_gain, mlp_gain, w_gate, w_up, w_down, doc_lengths
):
    row_count = hidden_in.shape[0]
    model_dim = hidden_in.shape[1]
    scale_score = 1.0 / math.sqrt(HEAD_DIM)
    doc_ids, positions, real_mask = layout(doc_lengths, row_count)
    real_rows = real_mask.astype(jnp.float32)
    cos_table, sin_table = rope_tables(positions)
    cos_heads = cos_table[:, None, :]
    sin_heads = sin_table[:, None, :]
    allowed = doc_ids[:, None] == doc_ids[None, :]
    full_qkv, full_out, gain_one, gain_two = (
        lax.all_gather(w_qkv, ("seq", "mlp"), axis=1, tiled=True),
        lax.all_gather(w_attn_out, ("seq", "mlp"), axis=1, tiled=True),
        lax.all_gather(attn_gain, ("seq", "mlp"), axis=0, tiled=True),
        lax.all_gather(mlp_gain, ("seq", "mlp"), axis=0, tiled=True),
    )
    gain_attn = gain_one.astype(jnp.float32)
    gain_mlp = gain_two.astype(jnp.float32)
    hidden_first = hidden_in.astype(jnp.float32)
    normed_one, inverse_one = standardize(hidden_first)
    input_one = (normed_one * gain_attn).astype(jnp.bfloat16)
    projected = jnp.dot(input_one, full_qkv, preferred_element_type=jnp.float32)
    split_qkv = projected.reshape(row_count, 3, HEADS, HEAD_DIM)
    query_rows = (split_qkv[:, 0] * cos_heads + rotate_half(split_qkv[:, 0]) * sin_heads).astype(
        jnp.bfloat16
    )
    key_rows = (split_qkv[:, 1] * cos_heads + rotate_half(split_qkv[:, 1]) * sin_heads).astype(
        jnp.bfloat16
    )
    value_rows = split_qkv[:, 2].astype(jnp.bfloat16)
    query_heads = jnp.swapaxes(query_rows, 0, 1)
    key_heads = jnp.swapaxes(key_rows, 0, 1)
    value_heads = jnp.swapaxes(value_rows, 0, 1)

    def head_forward(inputs):
        query_one, key_one, value_one = inputs
        scores = (
            jnp.einsum("qd,kd->qk", query_one, key_one, preferred_element_type=jnp.float32)
            * scale_score
        )
        masked = jnp.where(allowed, scores, -1e30)
        top_score = jnp.max(masked, axis=1, keepdims=True)
        weights = jnp.exp(masked - top_score)
        total = jnp.sum(weights, axis=1, keepdims=True)
        attention = (weights / total).astype(jnp.bfloat16)
        mixed_one = jnp.dot(attention, value_one, preferred_element_type=jnp.float32)
        return (mixed_one, top_score[:, 0] + jnp.log(total[:, 0]))

    mixed_heads, log_totals = lax.map(head_forward, (query_heads, key_heads, value_heads))
    mixed = jnp.swapaxes(mixed_heads, 0, 1).reshape(row_count, model_dim)
    attended = (mixed * real_rows[:, None]).astype(jnp.bfloat16)
    hidden_mid = hidden_first + jnp.dot(attended, full_out, preferred_element_type=jnp.float32)
    normed_two, inverse_two = standardize(hidden_mid)
    input_two = (normed_two * gain_mlp).astype(jnp.bfloat16)
    grad_top = cotangent.astype(jnp.float32) * real_rows[:, None]
    grad_low = grad_top.astype(jnp.bfloat16)
    group_input = lax.all_gather(input_two, "mlp", axis=0, tiled=True)
    gate_pre = jnp.dot(group_input, w_gate, preferred_element_type=jnp.float32)
    up_pre = jnp.dot(group_input, w_up, preferred_element_type=jnp.float32)
    inner = (gelu_exact(gate_pre) * up_pre).astype(jnp.bfloat16)
    inner_rows = inner
    ffn_out = lax.psum_scatter(
        jnp.dot(inner_rows, w_down, preferred_element_type=jnp.float32).astype(jnp.bfloat16),
        "mlp",
        scatter_dimension=0,
        tiled=True,
    ).astype(jnp.float32)
    layer_out = (hidden_mid + ffn_out).astype(jnp.bfloat16)
    piece = lax.all_gather(grad_low, "mlp", axis=0, tiled=True)
    inner_rows = inner
    down_total = lax.dot_general(
        inner_rows, piece, contract_rows, preferred_element_type=jnp.float32
    )
    grad_inner = lax.dot_general(piece, w_down, contract_cols, preferred_element_type=jnp.float32)
    gate_rows = gate_pre
    up_rows = up_pre
    grad_gate_rows, grad_up_rows = geglu_back(grad_inner, gate_rows, up_rows)
    grad_gate_part = lax.dot_general(
        group_input, grad_gate_rows, contract_rows, preferred_element_type=jnp.float32
    )
    grad_up_part = lax.dot_general(
        group_input, grad_up_rows, contract_rows, preferred_element_type=jnp.float32
    )
    gate_rows = grad_gate_rows
    up_rows = grad_up_rows
    grad_normed_two = lax.psum_scatter(
        (
            lax.dot_general(gate_rows, w_gate, contract_cols, preferred_element_type=jnp.float32)
            + lax.dot_general(up_rows, w_up, contract_cols, preferred_element_type=jnp.float32)
        ).astype(jnp.bfloat16),
        "mlp",
        scatter_dimension=0,
        tiled=True,
    ).astype(jnp.float32)
    grad_gate_sum, grad_up_sum, grad_down_sum = lax.psum(
        (grad_gate_part, grad_up_part, down_total), "seq"
    )
    grad_gain_mlp = jnp.sum(grad_normed_two * normed_two, axis=0)
    grad_mid = grad_top + norm_back(grad_normed_two, normed_two, inverse_two, gain_mlp)
    grad_mid_low = grad_mid.astype(jnp.bfloat16)
    grad_out_weight = lax.dot_general(
        attended, grad_mid_low, contract_rows, preferred_element_type=jnp.float32
    )
    full_qkv, full_out = (
        lax.all_gather(w_qkv, ("seq", "mlp"), axis=1, tiled=True),
        lax.all_gather(w_attn_out, ("seq", "mlp"), axis=1, tiled=True),
    )
    grad_attended = lax.dot_general(
        grad_mid_low, full_out, contract_cols, preferred_element_type=jnp.float32
    )
    grad_mixed = jnp.where(
        real_mask[:, None], grad_attended.astype(jnp.bfloat16), jnp.zeros((), jnp.bfloat16)
    )
    grad_heads = jnp.swapaxes(grad_mixed.reshape(row_count, HEADS, HEAD_DIM), 0, 1)

    def head_backward(inputs):
        query_one, key_one, value_one, grad_one, log_one = inputs
        scores = (
            jnp.einsum("qd,kd->qk", query_one, key_one, preferred_element_type=jnp.float32)
            * scale_score
        )
        attention = jnp.where(allowed, jnp.exp(scores - log_one[:, None]), 0.0)
        attention_low = attention.astype(jnp.bfloat16)
        grad_value = lax.dot_general(
            attention_low, grad_one, contract_rows, preferred_element_type=jnp.float32
        )
        grad_attention = jnp.einsum(
            "qd,kd->qk", grad_one, value_one, preferred_element_type=jnp.float32
        )
        row_terms = jnp.sum(attention * grad_attention, axis=1, keepdims=True)
        grad_scores = (attention * (grad_attention - row_terms)).astype(jnp.bfloat16)
        grad_query = jnp.dot(grad_scores, key_one, preferred_element_type=jnp.float32) * scale_score
        grad_key = (
            lax.dot_general(
                grad_scores, query_one, contract_rows, preferred_element_type=jnp.float32
            )
            * scale_score
        )
        return (grad_query, grad_key, grad_value)

    grad_query_heads, grad_key_heads, grad_value_heads = lax.map(
        head_backward, (query_heads, key_heads, value_heads, grad_heads, log_totals)
    )
    grad_query_rows = jnp.swapaxes(grad_query_heads, 0, 1)
    grad_key_rows = jnp.swapaxes(grad_key_heads, 0, 1)
    grad_value_rows = jnp.swapaxes(grad_value_heads, 0, 1)
    grad_query_pre = grad_query_rows * cos_heads + rotate_back(grad_query_rows * sin_heads)
    grad_key_pre = grad_key_rows * cos_heads + rotate_back(grad_key_rows * sin_heads)
    grad_projected = (
        jnp.stack([grad_query_pre, grad_key_pre, grad_value_rows], axis=1)
        .reshape(row_count, 3 * model_dim)
        .astype(jnp.bfloat16)
    )
    grad_qkv_weight = lax.dot_general(
        input_one, grad_projected, contract_rows, preferred_element_type=jnp.float32
    )
    grad_normed_one = lax.dot_general(
        grad_projected, full_qkv, contract_cols, preferred_element_type=jnp.float32
    )
    grad_gain_attn = jnp.sum(grad_normed_one * normed_one, axis=0)
    grad_hidden = (
        grad_mid + norm_back(grad_normed_one, normed_one, inverse_one, gain_attn)
    ).astype(jnp.bfloat16)
    grad_qkv, grad_attn_out, grad_attn_gain, grad_mlp_gain = (
        lax.psum_scatter(grad_qkv_weight, ("seq", "mlp"), scatter_dimension=1, tiled=True),
        lax.psum_scatter(grad_out_weight, ("seq", "mlp"), scatter_dimension=1, tiled=True),
        lax.psum_scatter(grad_gain_attn, ("seq", "mlp"), scatter_dimension=0, tiled=True),
        lax.psum_scatter(grad_gain_mlp, ("seq", "mlp"), scatter_dimension=0, tiled=True),
    )
    return (
        layer_out,
        grad_hidden,
        grad_qkv,
        grad_attn_out,
        grad_attn_gain,
        grad_mlp_gain,
        grad_gate_sum,
        grad_up_sum,
        grad_down_sum,
    )


def solution(mesh):
    in_specs = (
        P(("seq", "mlp"), None),
        P(("seq", "mlp"), None),
        P(None, ("seq", "mlp")),
        P(None, ("seq", "mlp")),
        P(("seq", "mlp")),
        P(("seq", "mlp")),
        P(None, "mlp"),
        P(None, "mlp"),
        P("mlp", None),
        P(("seq", "mlp"), None),
    )
    out_specs = (
        P(("seq", "mlp"), None),
        P(("seq", "mlp"), None),
        P(None, ("seq", "mlp")),
        P(None, ("seq", "mlp")),
        P(("seq", "mlp")),
        P(("seq", "mlp")),
        P(None, "mlp"),
        P(None, "mlp"),
        P("mlp", None),
    )
    return jax.shard_map(shards, mesh=mesh, in_specs=in_specs, out_specs=out_specs, check_vma=False)
```

profile of v0, /device:TPU:0, one launch (start us, length us, event | category | flops | bytes accessed | tf_op | source)
XLA Modules:
  0.0 1179.7 jit_solution(4366558932656733398)
XLA Ops:
  12.9 42.2 %all-reduce.6 = (bf16[768]{0:T(1024)(128)(2,1)S(1)}, bf16[768]{0:T(1024)(128)(2,1)S(1)}) all-reduce(bf16[768]{0:T(1024)(128)(2,1)S(1)} %dynamic-update-slice, bf16[768]{0:T(1024)(128)(2,1)S(1)} %dynamic-update-slice.1), channel_id=1, replica_groups=mesh['seq'=8,'mlp'=4] {'seq','mlp'}, use_global_device_ids=true, to_apply=%add | all-reduce | flops 1536 | bytes 6144
  60.6 13.1 %all-gather.5.cloned.1.call-done = bf16[768,2304]{0,1:T(8,128)(2,1)} async-done(((bf16[768,72]{0,1:T(8,128)(2,1)}), bf16[768,2304]{0,1:T(8,128)(2,1)}) %all-gather.5.cloned.1.call-update) | async-done | bytes 3538960 | tf_op jit(solution)/shard_map/all_gather | solution.py:93
  73.7 6.9 fusion.99
  86.1 4.6 copy.63
  101.8 114.7 %while.28 = (s32[]{:T(128)}, f32[12,1152,64]{1,2,0:T(8,128)}, f32[12,1152]{1,0:T(8,128)S(1)}, bf16[12,1152,64]{2,1,0:T(8,128)(2,1)}, bf16[12,1152,64]{2,1,0:T(8,...) while((s32[]{:T(128)}, f32[12,1152,64]{1,2,0:T(8,128)}, ...), condition=%wide.region_8.9_spmd.clone, body=%wide.region_5.8_spmd.clone.sunk | while | flops 351681408 | bytes 38412412 | solution.py:130
  216.6 4.9 fusion.87
  229.1 126.7 %all-gather.9.cloned.1.call-done = bf16[4608,768]{0,1:T(8,128)(2,1)} async-done(((bf16[1152,768]{0,1:T(8,128)(2,1)}), bf16[4608,768]{0,1:T(8,128)(2,1)}) %all-gather.9.cloned.1.call-update) | async-done | bytes 7077904 | tf_op jit(solution)/shard_map/all_gather | solution.py:138
  355.8 7.8 fusion.111
  368.2 116.1 %all-gather.11.cloned.1.call-done = bf16[4608,768]{0,1:T(8,128)(2,1)} async-done(((bf16[1152,768]{0,1:T(8,128)(2,1)}), bf16[4608,768]{0,1:T(8,128)(2,1)}) %all-gather.11.cloned.1.call-update) | async-done | bytes 7077904 | tf_op jit(solution)/shard_map/all_gather | solution.py:150
  484.2 9.3 multiply_convert_fusion.1
  497.4 7.2 add_convert_fusion
  506.3 5.9 convolution_convert_fusion
  513.8 7.1 fusion.108
  527.5 98.9 %reduce-scatter.15.cloned.1.call-done = bf16[1152,768]{1,0:T(8,128)(2,1)} async-done(((bf16[4608,768]{1,0:T(8,128)(2,1)}), bf16[1152,768]{1,0:T(8,128)(2,1)}) %reduce-scatter.15.cloned.1.call-update) | async-done | bytes 1769488
  634.3 118.4 %reduce-scatter.13.cloned.1.call-done = bf16[1152,768]{1,0:T(8,128)(2,1)} async-done(((bf16[4608,768]{1,0:T(8,128)(2,1)}), bf16[1152,768]{1,0:T(8,128)(2,1)}) %reduce-scatter.13.cloned.1.call-update) | async-done | bytes 1769488
  756.6 5.0 fusion.77
  770.7 158.2 %while.29 = (s32[]{:T(128)}, f32[12,1152,64]{1,2,0:T(8,128)}, f32[12,1152,64]{1,2,0:T(8,128)}, bf16[12,1152,64]{1,2,0:T(8,128)(2,1)}, bf16[12,1152,64]{2,1,0:T(8...) while((s32[]{:T(128)}, f32[12,1152,64]{1,2,0:T(8,128)}, ...), condition=%wide.region_17.18_spmd.clone, body=%wide.region_15.17_spmd.clone.sunk | while | flops 862763904 | bytes 42810480 | solution.py:222
  928.8 6.8 multiply_bitcast_fusion.1
  952.4 7.0 fusion.97
  959.4 10.9 fusion.73
  970.3 40.9 %all-reduce.4 = (f32[768]{0:T(1024)S(1)}, f32[768]{0:T(1024)S(1)}) all-reduce(f32[768]{0:T(1024)S(1)} %get-tuple-element.235, f32[768]{0:T(1024)S(1)} %get-tuple-element.233), channel_id=6, replica_groups=mesh['seq'=8,'mlp'=4] {'seq','mlp'}, use_global_device_ids=true, to_apply=%region_23.24.clone | all-reduce | flops 1536 | bytes 12288
  1012.4 5.5 fusion.72
  1024.2 18.5 %reduce-scatter.11.cloned.1.call-done = f32[768,24]{0,1:T(8,128)} async-done(((f32[768,768]{0,1:T(8,128)}), f32[768,24]{0,1:T(8,128)}) %reduce-scatter.11.cloned.1.call-update) | async-done | bytes 73744 | tf_op jit(solution)/shard_map/reduce_scatter | solution.py:247
  1042.7 125.0 %reduce-scatter.9.cloned.1.call-done = f32[768,72]{0,1:T(8,128)} async-done(((f32[768,2304]{0,1:T(8,128)}), f32[768,72]{0,1:T(8,128)}) %reduce-scatter.9.cloned.1.call-update) | async-done | bytes 221200 | tf_op jit(solution)/shard_map/reduce_scatter | solution.py:246
  (348 shorter events, 375.6 us)
Async XLA Ops:
  7.2 477.1 %copy-start = (bf16[288,768]{1,0:T(8,128)(2,1)S(1)}, bf16[288,768]{1,0:T(8,128)(2,1)}, u32[]{:S(2)}) copy-start(bf16[288,768]{1,0:T(8,128)(2,1)} %param.22) | copy-start | bytes 1327108
  7.2 66.5 %all-gather.5.cloned.1.call-start = ((), (), s32[]{:S(2)}) async-start(), calls=%async_computation.4 | async-start | bytes 3649536 | tf_op jit(solution)/shard_map/all_gather | solution.py:93
  7.9 213.5 %all-gather.7.cloned.1.call-start = ((), (), s32[]{:S(2)}) async-start(), calls=%async_computation.5 | async-start | bytes 1216512 | tf_op jit(solution)/shard_map/all_gather | solution.py:94
  8.7 347.2 %all-gather.9.cloned.1.call-start = ((), (), s32[]{:S(2)}) async-start(), calls=%async_computation.6 | async-start | bytes 8847360 | tf_op jit(solution)/shard_map/all_gather | solution.py:138
  8.8 46.3 %copy-start.36 = (s32[1,5]{1,0:T(1,128)S(1)}, s32[1,5]{1,0:T(1,128)}, u32[]{:S(2)}) copy-start(s32[1,5]{1,0:T(1,128)} %param.23) | copy-start | bytes 64
  11.5 209.9 %copy-start.7 = (bf16[1152,768]{0,1:T(8,128)(2,1)}, bf16[1152,768]{0,1:T(8,128)(2,1)S(1)}, u32[]{:S(2)}) copy-start(bf16[1152,768]{0,1:T(8,128)(2,1)S(1)} %copy.61) | copy-start | bytes 5308420
  11.9 68.8 %copy-start.26 = (f32[1152]{0:T(1024)}, f32[1152]{0:T(1024)S(1)}, u32[]{:S(2)}) copy-start(f32[1152]{0:T(1024)S(1)} %broadcast_multiply_fusion.5) | copy-start | bytes 13828
  12.4 68.2 %copy-start.28 = (f32[1152]{0:T(1024)}, f32[1152]{0:T(1024)S(1)}, u32[]{:S(2)}) copy-start(f32[1152]{0:T(1024)S(1)} %add_rsqrt_fusion.1) | copy-start | bytes 13828
  55.1 25.5 %copy-start.30 = (f32[768]{0:T(1024)}, f32[768]{0:T(1024)S(1)}, u32[]{:S(2)}) copy-start(f32[768]{0:T(1024)S(1)} %convert_element_type.98) | copy-start | bytes 9220
  60.6 23.0 %copy-start.18 = (f32[1152,64]{0,1:T(8,128)}, f32[1152,64]{0,1:T(8,128)S(1)}, u32[]{:S(2)}) copy-start(f32[1152,64]{0,1:T(8,128)S(1)} %get-tuple-element.316) | copy-start | bytes 884740
  60.6 23.0 %copy-start.20 = (f32[1152,64]{0,1:T(8,128)}, f32[1152,64]{0,1:T(8,128)S(1)}, u32[]{:S(2)}) copy-start(f32[1152,64]{0,1:T(8,128)S(1)} %get-tuple-element.317) | copy-start | bytes 884740
  226.8 129.1 %copy-start.23 = (bf16[768,288]{0,1:T(8,128)(2,1)S(1)}, bf16[768,288]{0,1:T(8,128)(2,1)}, u32[]{:S(2)}) copy-start(bf16[768,288]{0,1:T(8,128)(2,1)} %param.20) | copy-start | bytes 1327108
  228.5 255.7 %all-gather.11.cloned.1.call-start = ((), (), s32[]{:S(2)}) async-start(), calls=%async_computation.7 | async-start | bytes 8847360 | tf_op jit(solution)/shard_map/all_gather | solution.py:150
  229.1 134.6 %copy-start.24 = (bf16[768,288]{0,1:T(8,128)(2,1)S(1)}, bf16[768,288]{0,1:T(8,128)(2,1)}, u32[]{:S(2)}) copy-start(bf16[768,288]{0,1:T(8,128)(2,1)} %param.21) | copy-start | bytes 1327108
  229.1 397.4 %reduce-scatter.15.cloned.1.call-start = ((), (), s32[]{:S(2)}) async-start(), calls=%async_computation.11 | async-start | bytes 8847360
  504.6 248.1 %reduce-scatter.13.cloned.1.call-start = ((), (), s32[]{:S(2)}) async-start(), calls=%async_computation.10 | async-start | bytes 8847360
  512.3 511.9 %all-reduce.9.cloned.1.call-start = ((), (), s32[]{:S(2)}) async-start(), calls=%async_computation.12 | async-start | bytes 5308416 | tf_op jit(solution)/shard_map/psum | solution.py:176
  513.8 10.3 slice-start.2
  527.3 515.3 %reduce-scatter.11.cloned.1.call-start = ((), (), s32[]{:S(2)}) async-start(), calls=%async_computation.9 | async-start | bytes 2433024 | tf_op jit(solution)/shard_map/reduce_scatter | solution.py:247
  630.3 126.2 %copy-start.9 = (bf16[1152,768]{0,1:T(8,128)(2,1)S(1)}, bf16[1152,768]{0,1:T(8,128)(2,1)}, u32[]{:S(2)}) copy-start(bf16[1152,768]{0,1:T(8,128)(2,1)} %copy.67) | copy-start | bytes 5308420
  770.7 158.2 %copy-start.21 = (f32[1152,64]{0,1:T(8,128)S(1)}, f32[1152,64]{0,1:T(8,128)}, u32[]{:S(2)}) copy-start(f32[1152,64]{0,1:T(8,128)} %copy-done.20) | copy-start | bytes 884740
  942.4 225.2 %reduce-scatter.9.cloned.1.call-start = ((), (), s32[]{:S(2)}) async-start(), calls=%async_computation.8 | async-start | bytes 7299072 | tf_op jit(solution)/shard_map/reduce_scatter | solution.py:246
  1021.9 150.9 %copy-start.1 = (bf16[288,768]{1,0:T(8,128)(2,1)S(1)}, bf16[288,768]{1,0:T(8,128)(2,1)}, u32[]{:S(2)}) copy-start(bf16[288,768]{1,0:T(8,128)(2,1)} %param.22) | copy-start | bytes 1327108
  1024.2 147.7 %copy-start.25 = (f32[288,768]{1,0:T(8,128)S(1)}, f32[288,768]{1,0:T(8,128)}, u32[]{:S(2)}) copy-start(f32[288,768]{1,0:T(8,128)} %get-tuple-element.498) | copy-start | bytes 2654212
  (39 other events, 144.0 us)
Sparse Core Ops, SparseCore 0:
  10.8 62.8 all-gather.4
  76.5 52.7 all-gather.6
  228.6 127.1 all-gather.8
  357.8 126.3 all-gather.10
  504.7 121.6 reduce-scatter.14
  628.6 124.0 reduce-scatter.12
  757.5 66.1 all-reduce.8
  942.5 100.1 reduce-scatter.10
  1048.9 118.6 reduce-scatter.8
where the time goes:
time: 1190 us; the launch traced here: 1180 us
  waiting for transfers between devices  619 us (52%)
  matrix products  310 us (26%)
  local copies, waits for them, and re-layouts  89.8 us (8%)
  blocking collectives  83.1 us (7%)
  other arithmetic  62.2 us (5%)
  between operations  14.7 us (1%)
    unnamed x11, waiting for transfers between devices  219 us
    all_gather x1, waiting for transfers between devices, shards(): group_input = lax.all_gather(input_two, 'mlp', axis=0, tiled=True)  127 us
    reduce_scatter x1, waiting for transfers between devices, shards(): lax.psum_scatter(grad_qkv_weight, ('seq', 'mlp'), scatter_dimension=1, ti...  125 us
    all_gather x1, waiting for transfers between devices, shards(): piece = lax.all_gather(grad_low, 'mlp', axis=0, tiled=True)  116 us
    unnamed x2, blocking collectives  83.1 us
    dot_general x12, matrix products, head_forward(): jnp.dot(attention, value_one, preferred_element_type=jnp.float32)  51.7 us
    unnamed x102, local copies, waits for them, and re-layouts  48.1 us
    dot_general x12, matrix products, head_backward(): jnp.einsum('qd,kd->qk', query_one, key_one, preferred_element_type=jnp.fl...  37.1 us
  transfers between devices with their start and end apart: 9, of which 7 were waited for; matrix products, arithmetic and copies ran while one was open for 34% of the time, Pallas kernels for 0%

commit v1 on v0

v1 whole, which is shorter than its diff:
```python
import math

import jax
import jax.numpy as jnp
from jax import lax
from jax.sharding import PartitionSpec as P

HEADS = 12
HEAD_DIM = 64


eps_norm = 1e-05
theta_rope = 160000.0
contract_rows = (((0,), (0,)), ((), ()))
contract_cols = (((1,), (1,)), ((), ()))
bf16 = jnp.bfloat16
f32 = jnp.float32


def layout(doc_lengths, row_count):
    lengths = doc_lengths[0]
    slot_count = lengths.shape[0]
    doc_ends = jnp.cumsum(lengths)
    starts = doc_ends - lengths
    places = jnp.arange(row_count, dtype=jnp.int32)
    doc_ids = jnp.sum((places[:, None] >= doc_ends[None, :]).astype(jnp.int32), axis=1)
    picked = doc_ids[:, None] == jnp.arange(slot_count, dtype=jnp.int32)[None, :]
    offsets = jnp.sum(jnp.where(picked, starts[None, :], 0), axis=1)
    return (doc_ids, places - offsets, doc_ids < slot_count - 1)


def rope_tables(positions):
    half_dim = HEAD_DIM // 2
    frequency = jnp.exp(
        jnp.arange(half_dim, dtype=jnp.float32) * (-2.0 * math.log(theta_rope) / HEAD_DIM)
    )
    angles = positions.astype(jnp.float32)[..., None] * frequency
    cos_table = jnp.concatenate([jnp.cos(angles), jnp.cos(angles)], axis=-1)
    sin_table = jnp.concatenate([jnp.sin(angles), jnp.sin(angles)], axis=-1)
    return (cos_table, sin_table)


def rotate_half(vector):
    half_dim = vector.shape[-1] // 2
    return jnp.concatenate([-vector[..., half_dim:], vector[..., :half_dim]], axis=-1)


def rotate_back(vector):
    half_dim = vector.shape[-1] // 2
    return jnp.concatenate([vector[..., half_dim:], -vector[..., :half_dim]], axis=-1)


def standardize(value):
    mean_value = jnp.mean(value, axis=-1, keepdims=True)
    centered = value - mean_value
    inverse = lax.rsqrt(jnp.mean(centered * centered, axis=-1, keepdims=True) + eps_norm)
    return (centered * inverse, inverse)


def norm_back(grad_normed, normed, inverse, gain):
    scaled = grad_normed * gain
    return inverse * (
        scaled
        - jnp.mean(scaled, axis=-1, keepdims=True)
        - normed * jnp.mean(scaled * normed, axis=-1, keepdims=True)
    )


def gelu_exact(value):
    return 0.5 * value * (1.0 + lax.erf(value * (1.0 / math.sqrt(2.0))))


def geglu_back(grad_inner, gate_pre, up_pre):
    cumulative = 0.5 * (1.0 + lax.erf(gate_pre * (1.0 / math.sqrt(2.0))))
    density = jnp.exp(-0.5 * gate_pre * gate_pre) * (1.0 / math.sqrt(2.0 * math.pi))
    slope = cumulative + gate_pre * density
    grad_gate = (grad_inner * up_pre * slope).astype(jnp.bfloat16)
    grad_up = (grad_inner * (gate_pre * cumulative)).astype(jnp.bfloat16)
    return (grad_gate, grad_up)


class Links:
    def __init__(self, seq_size, mlp_size):
        self.seq_size, self.mlp_size = seq_size, mlp_size
        self.seq, self.mlp = lax.axis_index("seq"), lax.axis_index("mlp")
        self.seq_bits = seq_size.bit_length() - 1
        self.mlp_bits = mlp_size.bit_length() - 1
        self.low = self.seq & 1

    def stages(self, bits):
        upper = list(range(1, bits))
        out = []
        while len(upper) >= 2:
            one, two = upper[0], upper[1]
            out += [(two, one), (one, two)]
            upper = upper[2:]
        return out + [(bit, bit) for bit in upper]

    def swap_seq(self, value, even_bit, odd_bit):
        pairs = [(i, i ^ (1 << (odd_bit if i & 1 else even_bit))) for i in range(self.seq_size)]
        return lax.ppermute(value, "seq", pairs)

    def swap_mlp(self, value, bit):
        pairs = [(i, i ^ (1 << bit)) for i in range(self.mlp_size)]
        return lax.ppermute(value, "mlp", pairs)

    def seq_bit(self, even_bit, odd_bit):
        return (self.seq >> jnp.where(self.low == 1, odd_bit, even_bit)) & 1

    @staticmethod
    def pair(mine, other, bit):
        first = jnp.where(bit == 0, mine, other)
        second = jnp.where(bit == 0, other, mine)
        return jnp.stack([first, second])

    def absolute(self, bits, which):
        return [stage[which] for stage in reversed(self.stages(bits))]

    def gather(self, unit, bits):
        shape = unit.shape
        value = unit
        for bit in range(self.mlp_bits):
            value = self.pair(value, self.swap_mlp(value, bit), (self.mlp >> bit) & 1)
        value = value.reshape((self.mlp_size,) + shape)
        for even_bit, odd_bit in self.stages(bits):
            other = self.swap_seq(value, even_bit, odd_bit)
            value = self.pair(value, other, self.seq_bit(even_bit, odd_bit))
        other = self.swap_seq(value, 0, 0)
        halves = self.pair(value, other, self.low)
        sorted_halves = []
        for which in (0, 1):
            order = self.absolute(bits, which)
            places = [order.index(bit) for bit in range(bits - 1, 0, -1)]
            rest = list(range(len(order), len(order) + 1 + len(shape)))
            sorted_halves.append(jnp.transpose(halves[which], places + rest))
        return jnp.stack(sorted_halves, axis=bits - 1).reshape((1 << bits, self.mlp_size) + shape)

    def scatter_sum(self, value, bits):
        shape = value.shape[2:]
        value = value.reshape((2,) * bits + (self.mlp_size,) + shape)
        halves = []
        for which in (0, 1):
            half = lax.index_in_dim(value, which, bits - 1, keepdims=False)
            order = self.absolute(bits, which)
            rest = list(range(bits - 1, bits - 1 + 1 + len(shape)))
            halves.append(jnp.transpose(half, [bits - 1 - bit for bit in order] + rest))
        mine = jnp.where(self.low == 0, halves[0], halves[1])
        away = jnp.where(self.low == 0, halves[1], halves[0]).astype(bf16)
        value = mine + self.swap_seq(away, 0, 0).astype(f32)
        for even_bit, odd_bit in reversed(self.stages(bits)):
            bit = self.seq_bit(even_bit, odd_bit)
            mine = jnp.where(bit == 0, value[0], value[1])
            away = jnp.where(bit == 0, value[1], value[0]).astype(bf16)
            value = mine + self.swap_seq(away, even_bit, odd_bit).astype(f32)
        value = value.reshape((2,) * self.mlp_bits + shape)
        for bit in reversed(range(self.mlp_bits)):
            own = (self.mlp >> bit) & 1
            mine = jnp.where(own == 0, value[0], value[1])
            away = jnp.where(own == 0, value[1], value[0]).astype(bf16)
            value = mine + self.swap_mlp(away, bit).astype(f32)
        return value

    def total(self, value):
        for bit in range(self.seq_bits):
            value = value + self.swap_seq(value, bit, bit)
        for bit in range(self.mlp_bits):
            value = value + self.swap_mlp(value, bit)
        return value


def after(value, *others):
    return lax.optimization_barrier((value,) + others)[0]


def pad_rows(value, rows):
    return jnp.pad(value, ((0, rows - value.shape[0]), (0, 0)))


def up_to(value, step):
    return -(-value // step) * step


def make_shards(seq_size, mlp_size):
    def shards(
        hidden_in,
        cotangent,
        w_qkv,
        w_attn_out,
        attn_gain,
        mlp_gain,
        w_gate,
        w_up,
        w_down,
        doc_lengths,
    ):
        links = Links(seq_size, mlp_size)
        devices = seq_size * mlp_size
        row_count = hidden_in.shape[0]
        model_dim = hidden_in.shape[1]
        units = w_down.shape[0]
        hidden_units = units * mlp_size
        scale_score = 1.0 / math.sqrt(HEAD_DIM)

        qkv_part = w_qkv.shape[1]
        out_part = w_attn_out.shape[1]
        gain_part = attn_gain.shape[0]
        qkv_rows = up_to(qkv_part + 1, 16)
        gains = jnp.concatenate([attn_gain, mlp_gain])
        gains = jnp.pad(gains, (0, model_dim - gains.shape[0]))
        unit_qkv = pad_rows(jnp.concatenate([w_qkv.T, gains[None]]), qkv_rows)
        all_qkv = links.gather(unit_qkv, links.seq_bits).reshape(devices, qkv_rows, model_dim)
        full_qkv = all_qkv[:, :qkv_part].reshape(3 * model_dim, model_dim)
        gain_rows = all_qkv[:, qkv_part]
        gain_attn = gain_rows[:, :gain_part].reshape(model_dim).astype(f32)
        gain_mlp = gain_rows[:, gain_part : 2 * gain_part].reshape(model_dim).astype(f32)

        share_bits = min(3, links.seq_bits)
        shares = 1 << share_bits
        share_rows = up_to(up_to(3 * units, shares) // shares, 16)
        local_ff = pad_rows(jnp.concatenate([w_gate.T, w_up.T, w_down]), share_rows * shares)
        unit_ff = lax.dynamic_slice_in_dim(
            local_ff, (links.seq % shares) * share_rows, share_rows, axis=0
        )
        unit_out = pad_rows(w_attn_out.T, up_to(out_part, 16))
        unit_out = after(unit_out, full_qkv)
        all_out = links.gather(unit_out, links.seq_bits)
        full_out = all_out.reshape((devices,) + unit_out.shape)[:, :out_part]
        full_out = full_out.reshape(model_dim, model_dim)
        unit_ff = after(unit_ff, full_out)
        all_ff = jnp.swapaxes(links.gather(unit_ff, share_bits), 0, 1)
        all_ff = all_ff.reshape(mlp_size, share_rows * shares, model_dim)
        full_gate = all_ff[:, :units].reshape(hidden_units, model_dim)
        full_up = all_ff[:, units : 2 * units].reshape(hidden_units, model_dim)
        full_down = all_ff[:, 2 * units : 3 * units].reshape(hidden_units, model_dim)

        doc_ids, positions, real_mask = layout(doc_lengths, row_count)
        real_rows = real_mask.astype(jnp.float32)
        cos_table, sin_table = rope_tables(positions)
        cos_heads = cos_table[:, None, :]
        sin_heads = sin_table[:, None, :]
        allowed = doc_ids[:, None] == doc_ids[None, :]
        hidden_first = hidden_in.astype(jnp.float32)
        normed_one, inverse_one = standardize(hidden_first)
        input_one = (normed_one * gain_attn).astype(jnp.bfloat16)
        projected = lax.dot_general(
            input_one, full_qkv, contract_cols, preferred_element_type=jnp.float32
        )
        split_qkv = projected.reshape(row_count, 3, HEADS, HEAD_DIM)
        query_rows = (
            split_qkv[:, 0] * cos_heads + rotate_half(split_qkv[:, 0]) * sin_heads
        ).astype(jnp.bfloat16)
        key_rows = (split_qkv[:, 1] * cos_heads + rotate_half(split_qkv[:, 1]) * sin_heads).astype(
            jnp.bfloat16
        )
        value_rows = split_qkv[:, 2].astype(jnp.bfloat16)
        query_heads = jnp.swapaxes(query_rows, 0, 1)
        key_heads = jnp.swapaxes(key_rows, 0, 1)
        value_heads = jnp.swapaxes(value_rows, 0, 1)

        def head_forward(inputs):
            query_one, key_one, value_one = inputs
            scores = (
                jnp.einsum("qd,kd->qk", query_one, key_one, preferred_element_type=jnp.float32)
                * scale_score
            )
            masked = jnp.where(allowed, scores, -1e30)
            top_score = jnp.max(masked, axis=1, keepdims=True)
            weights = jnp.exp(masked - top_score)
            total = jnp.sum(weights, axis=1, keepdims=True)
            attention = (weights / total).astype(jnp.bfloat16)
            mixed_one = jnp.dot(attention, value_one, preferred_element_type=jnp.float32)
            return (mixed_one, top_score[:, 0] + jnp.log(total[:, 0]))

        mixed_heads, log_totals = lax.map(head_forward, (query_heads, key_heads, value_heads))
        mixed = jnp.swapaxes(mixed_heads, 0, 1).reshape(row_count, model_dim)
        attended = (mixed * real_rows[:, None]).astype(jnp.bfloat16)
        hidden_mid = hidden_first + lax.dot_general(
            attended, full_out, contract_cols, preferred_element_type=jnp.float32
        )
        normed_two, inverse_two = standardize(hidden_mid)
        input_two = (normed_two * gain_mlp).astype(jnp.bfloat16)
        grad_top = cotangent.astype(jnp.float32) * real_rows[:, None]
        grad_low = grad_top.astype(jnp.bfloat16)

        gate_pre = lax.dot_general(input_two, full_gate, contract_cols, preferred_element_type=f32)
        up_pre = lax.dot_general(input_two, full_up, contract_cols, preferred_element_type=f32)
        inner = (gelu_exact(gate_pre) * up_pre).astype(jnp.bfloat16)
        ffn_out = jnp.dot(inner, full_down, preferred_element_type=jnp.float32)
        layer_out = (hidden_mid + ffn_out).astype(jnp.bfloat16)
        down_part = lax.dot_general(inner, grad_low, contract_rows, preferred_element_type=f32)
        grad_inner = lax.dot_general(grad_low, full_down, contract_cols, preferred_element_type=f32)
        grad_gate_rows, grad_up_rows = geglu_back(grad_inner, gate_pre, up_pre)
        gate_part = lax.dot_general(
            grad_gate_rows, input_two, contract_rows, preferred_element_type=f32
        )
        up_part = lax.dot_general(grad_up_rows, input_two, contract_rows, preferred_element_type=f32)
        grad_normed_two = jnp.dot(grad_gate_rows, full_gate, preferred_element_type=f32) + jnp.dot(
            grad_up_rows, full_up, preferred_element_type=f32
        )
        grads_ff = jnp.concatenate(
            [
                part.astype(bf16).reshape(mlp_size, units, model_dim)
                for part in (gate_part, up_part, down_part)
            ],
            axis=1,
        )
        seq_rows = up_to(3 * units, seq_size * 16) // seq_size
        grads_ff = jnp.pad(grads_ff, ((0, 0), (0, seq_rows * seq_size - 3 * units), (0, 0)))
        grads_ff = jnp.swapaxes(
            grads_ff.reshape(mlp_size, seq_size, seq_rows, model_dim), 0, 1
        ).reshape(seq_size * mlp_size * seq_rows, model_dim)
        grads_ff = lax.psum_scatter(grads_ff, "seq", scatter_dimension=0, tiled=True)
        grads_ff = lax.psum_scatter(grads_ff, "mlp", scatter_dimension=0, tiled=True)
        grads_ff = lax.all_gather(grads_ff, "seq", axis=0, tiled=True).astype(f32)
        grad_gate_sum = grads_ff[:units].T
        grad_up_sum = grads_ff[units : 2 * units].T
        grad_down_sum = grads_ff[2 * units : 3 * units]

        grad_gain_mlp = jnp.sum(grad_normed_two * normed_two, axis=0)
        grad_mid = grad_top + norm_back(grad_normed_two, normed_two, inverse_two, gain_mlp)
        grad_mid_low = grad_mid.astype(jnp.bfloat16)
        out_grad = lax.dot_general(
            grad_mid_low, attended, contract_rows, preferred_element_type=jnp.float32
        )
        grad_attn_out = links.scatter_sum(
            out_grad.reshape(seq_size, mlp_size, out_part, model_dim), links.seq_bits
        ).T
        grad_attended = jnp.dot(grad_mid_low, full_out, preferred_element_type=jnp.float32)
        grad_mixed = jnp.where(
            real_mask[:, None], grad_attended.astype(jnp.bfloat16), jnp.zeros((), jnp.bfloat16)
        )
        grad_heads = jnp.swapaxes(grad_mixed.reshape(row_count, HEADS, HEAD_DIM), 0, 1)

        def head_backward(inputs):
            query_one, key_one, value_one, grad_one, log_one = inputs
            scores = (
                jnp.einsum("qd,kd->qk", query_one, key_one, preferred_element_type=jnp.float32)
                * scale_score
            )
            attention = jnp.where(allowed, jnp.exp(scores - log_one[:, None]), 0.0)
            attention_low = attention.astype(jnp.bfloat16)
            grad_value = lax.dot_general(
                attention_low, grad_one, contract_rows, preferred_element_type=jnp.float32
            )
            grad_attention = jnp.einsum(
                "qd,kd->qk", grad_one, value_one, preferred_element_type=jnp.float32
            )
            row_terms = jnp.sum(attention * grad_attention, axis=1, keepdims=True)
            grad_scores = (attention * (grad_attention - row_terms)).astype(jnp.bfloat16)
            grad_query = (
                jnp.dot(grad_scores, key_one, preferred_element_type=jnp.float32) * scale_score
            )
            grad_key = (
                lax.dot_general(
                    grad_scores, query_one, contract_rows, preferred_element_type=jnp.float32
                )
                * scale_score
            )
            return (grad_query, grad_key, grad_value)

        grad_query_heads, grad_key_heads, grad_value_heads = lax.map(
            head_backward, (query_heads, key_heads, value_heads, grad_heads, log_totals)
        )
        grad_query_rows = jnp.swapaxes(grad_query_heads, 0, 1)
        grad_key_rows = jnp.swapaxes(grad_key_heads, 0, 1)
        grad_value_rows = jnp.swapaxes(grad_value_heads, 0, 1)
        grad_query_pre = grad_query_rows * cos_heads + rotate_back(grad_query_rows * sin_heads)
        grad_key_pre = grad_key_rows * cos_heads + rotate_back(grad_key_rows * sin_heads)
        grad_projected = (
            jnp.stack([grad_query_pre, grad_key_pre, grad_value_rows], axis=1)
            .reshape(row_count, 3 * model_dim)
            .astype(jnp.bfloat16)
        )
        qkv_grad = lax.dot_general(
            grad_projected, input_one, contract_rows, preferred_element_type=jnp.float32
        )
        grad_qkv = links.scatter_sum(
            qkv_grad.reshape(seq_size, mlp_size, qkv_part, model_dim), links.seq_bits
        ).T
        grad_normed_one = jnp.dot(grad_projected, full_qkv, preferred_element_type=jnp.float32)
        grad_gain_attn = jnp.sum(grad_normed_one * normed_one, axis=0)
        grad_hidden = (
            grad_mid + norm_back(grad_normed_one, normed_one, inverse_one, gain_attn)
        ).astype(jnp.bfloat16)
        gain_grads = links.total(jnp.stack([grad_gain_attn, grad_gain_mlp]))
        own_gain = (links.seq * mlp_size + links.mlp) * gain_part
        gain_grads = lax.dynamic_slice_in_dim(gain_grads, own_gain, gain_part, axis=1)
        return (
            layer_out,
            grad_hidden,
            grad_qkv,
            grad_attn_out,
            gain_grads[0],
            gain_grads[1],
            grad_gate_sum,
            grad_up_sum,
            grad_down_sum,
        )

    return shards


def solution(mesh):
    both = ("seq", "mlp")
    in_specs = (
        P(both, None),
        P(both, None),
        P(None, both),
        P(None, both),
        P(both),
        P(both),
        P(None, "mlp"),
        P(None, "mlp"),
        P("mlp", None),
        P(both, None),
    )
    out_specs = (
        P(both, None),
        P(both, None),
        P(None, both),
        P(None, both),
        P(both),
        P(both),
        P(None, "mlp"),
        P(None, "mlp"),
        P("mlp", None),
    )
    body = make_shards(mesh.shape["seq"], mesh.shape["mlp"])
    return jax.shard_map(body, mesh=mesh, in_specs=in_specs, out_specs=out_specs, check_vma=False)
```

time: 1190 us -> 609 us (0.51)
  waiting for transfers between devices: 619 us -> 100 us
  blocking collectives: 83.1 us -> 0 us
  matrix products: 310 us -> 257 us
  starting transfers between devices: 0.75 us -> 35.5 us
  other arithmetic: 62.2 us -> 87.6 us
  local copies, waits for them, and re-layouts: 89.8 us -> 103 us
    all_gather x4 -> x1, waiting for transfers between devices: 256 us -> 0.01 us  [shards(): grads_ff = lax.all_gather(grads_ff, 'seq', axis=0, tiled=True).astype(f32)]
    unnamed x11 -> x3, waiting for transfers between devices: 219 us -> 0.05 us
    reduce_scatter x2, waiting for transfers between devices: 143 us -> 0.01 us  [the longest x1 0.01 us: shards(): lax.psum_scatter(grads_ff, 'seq', scatter_dimension=0, tiled=True)]
    ppermute x0 -> x30, waiting for transfers between devices: none -> 100 us  [the longest x18 54.4 us: swap_seq(): return lax.ppermute(value, 'seq', pairs)]
    unnamed x2 -> x0, blocking collectives: 83.1 us -> none
    ppermute x0 -> x30, starting transfers between devices: none -> 35.3 us  [the longest x12 19 us: swap_mlp(): return lax.ppermute(value, 'mlp', pairs)]
    while x24 -> x0, local copies, waits for them, and re-layouts: 28.1 us -> none
    dot_general x12, matrix products: 51.7 us -> 23.9 us  [head_forward(): jnp.dot(attention, value_one, preferred_element_type=jnp.float32)]
  transfers between devices with their start and end apart: 9 -> 33, of which waited for: 7 -> 18; matrix products, arithmetic and copies ran while one was open for 34% -> 59% of each run, Pallas kernels for 0% -> 0%
where the time goes in v1:
time: 609 us; the launch traced here: 599 us
  matrix products  257 us (42%)
  local copies, waits for them, and re-layouts  103 us (17%)
  waiting for transfers between devices  100 us (16%)
  other arithmetic  87.6 us (14%)
  starting transfers between devices  35.5 us (6%)
  between operations  15.3 us (3%)
    ppermute x18, waiting for transfers between devices, swap_seq(): return lax.ppermute(value, 'seq', pairs)  54.4 us
    ppermute x12, waiting for transfers between devices, swap_mlp(): return lax.ppermute(value, 'mlp', pairs)  45.8 us
    unnamed x123, local copies, waits for them, and re-layouts  39.5 us
    dot_general x12, matrix products, head_backward(): jnp.einsum('qd,kd->qk', query_one, key_one, preferred_element_type=jnp.fl...  37.2 us
    dot_general x12, matrix products, head_backward(): lax.dot_general(grad_scores, query_one, contract_rows, preferred_element_...  31.2 us
    dot_general x12, matrix products, head_backward(): lax.dot_general(attention_low, grad_one, contract_rows, preferred_element...  30.7 us
    dot_general x12, matrix products, head_backward(): jnp.dot(grad_scores, key_one, preferred_element_type=jnp.float32)  27 us
    dot_general x12, matrix products, head_forward(): jnp.dot(attention, value_one, preferred_element_type=jnp.float32)  23.9 us
  transfers between devices with their start and end apart: 33, of which 18 were waited for; matrix products, arithmetic and copies ran while one was open for 59% of the time, Pallas kernels for 0%

profile of v1, /device:TPU:0, one launch (start us, length us, event | category | flops | bytes accessed | tf_op | source)
XLA Modules:
  0.0 599.3 jit_solution(5688482571461705366)
XLA Ops:
  19.1 10.5 %collective-permute-done.1 = bf16[2,80,768]{2,1,0:T(8,128)(2,1)S(1)} collective-permute-done((bf16[2,80,768]{2,1,0:T(8,128)(2,1)S(1)}, bf16[2,80,768]{2,1,0:T(8,128)(2,1)S(1)}, u32[]{:S(2)}, u32[]{:S(2)}) %collective-permute-start.1) | collective-permute-done | bytes 245792 | tf_op jit(solution)/shard_map/ppermute | solution.py:105
  31.5 7.4 %collective-permute-done.2 = bf16[4,80,768]{2,0,1:T(4,128)(2,1)S(1)} collective-permute-done((bf16[4,80,768]{2,0,1:T(4,128)(2,1)S(1)}, bf16[4,80,768]{2,0,1:T(4,128)(2,1)S(1)}, u32[]{:S(2)}, u32[]{:S(2)}) %collective-permute-start.2) | collective-permute-done | bytes 491552 | tf_op jit(solution)/shard_map/ppermute | solution.py:101
  41.5 12.8 %collective-permute-done.3 = bf16[2,4,80,768]{3,1,0,2:T(4,128)(2,1)} collective-permute-done((bf16[2,4,80,768]{3,1,0,2:T(4,128)(2,1)S(1)}, bf16[2,4,80,768]{3,1,0,2:T(4,128)(2,1)}, u32[]{:S(2)}, u32[]{:S(2)}) %collective-permute-start.3) | collective-permute-done | bytes 983072 | tf_op jit(solution)/shard_map/ppermute | solution.py:101
  68.0 4.5 pad_maximum_fusion.1
  72.5 7.2 %reshape_reshape.8 = bf16[32,80,768]{2,0,1:T(8,128)(2,1)} reshape(bf16[2,2,2,4,80,768]{5,3,2,1,0,4:T(4,128)(2,1)} %pad_maximum_fusion.1) | data formatting | bytes 7864320 | tf_op jit(solution)/shard_map/reshape;reshape | solution.py:211
  92.4 4.6 collective-permute-done.6
  105.2 5.5 collective-permute-done.8
  112.1 4.2 copy.124
  123.6 5.2 fusion.91
  136.0 11.8 %collective-permute-done.11 = bf16[2,112,768]{2,1,0:T(8,128)(2,1)S(1)} collective-permute-done((bf16[2,112,768]{2,1,0:T(8,128)(2,1)S(1)}, bf16[2,112,768]{2,1,0:T(8,128)(2,1)S(1)}, u32[]{:S(2)}, u32[]{:S(2)}) %collective-permute-start.11) | collective-permute-done | bytes 344096 | tf_op jit(solution)/shard_map/ppermute | solution.py:105
  153.1 5.9 collective-permute-done.12
  170.7 8.4 %collective-permute-done.13 = bf16[2,4,112,768]{3,2,1,0:T(8,128)(2,1)} collective-permute-done((bf16[2,4,112,768]{3,2,1,0:T(8,128)(2,1)}, bf16[2,4,112,768]{3,2,1,0:T(8,128)(2,1)}, u32[]{:S(2)}, u32[]{:S(2)}) %collective-permute-start.13) | collective-permute-done | bytes 1376288 | tf_op jit(solution)/shard_map/ppermute | solution.py:101
  183.2 74.0 %while.28 = (s32[]{:T(128)}, f32[12,1152,64]{1,2,0:T(8,128)S(1)}, f32[12,1152]{1,0:T(8,128)}, bf16[12,1152,64]{2,1,0:T(8,128)(2,1)}, bf16[12,1152,64]{2,1,0:T(8,...) while((s32[]{:T(128)}, f32[12,1152,64]{1,2,0:T(8,128)S(1)}, ...), condition=%wide.region_8.9_spmd.clone, body=%wide.region_5.8_spmd.clone.sunk | while | flops 351681408 | bytes 17185896 | solution.py:274
  274.1 6.0 %multiply_convert_fusion.1 = (bf16[1152,1152]{1,0:T(8,128)(2,1)S(1)}, bf16[1152,1152]{1,0:T(8,128)(2,1)S(1)}, bf16[1152,1152]{1,0:T(8,128)(2,1)}) fusion(f32[1152,1152]{1,0:T(8,128)S(1)} %fusion.127, f32[1152,1152]{1,0:T(8,128)S(1)} %fusion.128, bf16[1152,768]{1,0:T(8,128)(2,1)S(1)} %bitcast.361, bf16[1152,768]{0,1:T(8,128)(2,1)S(1)} %copy-done.7, ...), kind=kOutput, calls=%fused_computation.71 | convolution fusion | flops 2064973824 | bytes 22123008 | tf_op jit(solution)/shard_map/dot_general | solution.py:291
  284.3 4.7 fusion.129
  294.1 5.8 multiply_reduce_fusion.1
  316.5 4.7 copy.125
  325.5 167.1 %while.29 = (s32[]{:T(128)}, f32[12,1152,64]{1,2,0:T(8,128)}, f32[12,1152,64]{1,2,0:T(8,128)}, bf16[12,1152,64]{1,2,0:T(8,128)(2,1)}, bf16[12,1152,64]{2,1,0:T(8...) while((s32[]{:T(128)}, f32[12,1152,64]{1,2,0:T(8,128)}, ...), condition=%wide.region_15.16_spmd.clone, body=%wide.region_13.15_spmd.clone.sunk | while | flops 862763904 | bytes 42810488 | solution.py:361
  503.6 6.1 %fusion.75 = (f32[768]{0:T(1024)S(1)}, f32[1152]{0:T(1024)S(1)}, f32[1152]{0:T(1024)S(1)}, f32[1152,768]{0,1:T(8,128)S(1)}) fusion(bf16[1152,768]{0,1:T(8,128)(2,1)S(1)} %copy-done.3, f32[1152]{0:T(1024)S(1)} %copy-done.48, f32[1152]{0:T(1024)S(1)} %copy-done.40, f32[768]{0:T(1024)S(1)} %copy-done.50, bf16[1152,2304]{0,1:T(8,128)(2,1)S(1)} %bitcast.350, ...), kind=kOutput, calls=%fused_computation.92 | convolution fusion | flops 4084823040 | bytes 14180352 | tf_op jit(solution)/shard_map/dot_general | solution.py:380
  509.8 5.1 fusion.89
  526.6 4.2 fusion.74
  540.5 6.2 %fusion.84 = bf16[1152,768]{0,1:T(8,128)(2,1)} fusion(f32[1152,768]{0,1:T(8,128)S(1)} %get-tuple-element.361, bf16[1152,1152]{1,0:T(8,128)(2,1)} %get-tuple-element.304, bf16[1152,768]{1,0:T(8,128)(2,1)} %bitcast.362), kind=kOutput, calls=%fused_computation.121 | convolution fusion | flops 2040201216 | bytes 9732096 | tf_op jit(solution)/shard_map/dot_general | solution.py:288
  566.1 6.2 %collective-permute-done.17 = bf16[4,72,768]{2,1,0:T(8,128)(2,1)S(1)} collective-permute-done((bf16[4,72,768]{2,1,0:T(8,128)(2,1)S(1)}, bf16[4,72,768]{2,1,0:T(8,128)(2,1)S(1)}, u32[]{:S(2)}, u32[]{:S(2)}) %collective-permute-start.17) | collective-permute-done | bytes 442400 | tf_op jit(solution)/shard_map/ppermute | solution.py:101
  575.1 7.6 %collective-permute-done.18 = bf16[2,72,768]{2,1,0:T(8,128)(2,1)S(1)} collective-permute-done((bf16[2,72,768]{2,1,0:T(8,128)(2,1)S(1)}, bf16[2,72,768]{2,1,0:T(8,128)(2,1)S(1)}, u32[]{:S(2)}, u32[]{:S(2)}) %collective-permute-start.18) | collective-permute-done | bytes 221216 | tf_op jit(solution)/shard_map/ppermute | solution.py:105
  (462 shorter events, 438.5 us)
Async XLA Ops:
  7.2 533.2 %reduce-scatter.3.cloned.1.call-start = ((), (), s32[]{:S(2)}) async-start(), calls=%async_computation.2 | async-start | bytes 6193152 | tf_op jit(solution)/shard_map/reduce_scatter | solution.py:312
  16.3 13.4 %collective-permute-start.1 = (bf16[2,80,768]{2,1,0:T(8,128)(2,1)S(1)}, bf16[2,80,768]{2,1,0:T(8,128)(2,1)S(1)}, u32[]{:S(2)}, u32[]{:S(2)}) collective-permute-start(bf16[2,80,768]{2,1,0:T(8,128)(2,1)S(1)} %pad_maximum_fusion.14), channel_id=1, source_target_pairs={{0,2},{1,3},{2,0},{3,1},{4,6},{5,7},{6,4},{7,5},{8,10},{9,11},{10,... | collective-permute-start | bytes 737288 | tf_op jit(solution)/shard_map/ppermute | solution.py:105
  30.0 8.9 %collective-permute-start.2 = (bf16[4,80,768]{2,0,1:T(4,128)(2,1)S(1)}, bf16[4,80,768]{2,0,1:T(4,128)(2,1)S(1)}, u32[]{:S(2)}, u32[]{:S(2)}) collective-permute-start(bf16[4,80,768]{2,0,1:T(4,128)(2,1)S(1)} %copy.109), channel_id=1, source_target_pairs={{0,16},{4,12},{8,24},{12,4},{16,0},{20,28},{24,8},{28,20},{1,17},{... | collective-permute-start | bytes 1474568 | tf_op jit(solution)/shard_map/ppermute | solution.py:101
  40.1 14.3 %collective-permute-start.3 = (bf16[2,4,80,768]{3,1,0,2:T(4,128)(2,1)S(1)}, bf16[2,4,80,768]{3,1,0,2:T(4,128)(2,1)}, u32[]{:S(2)}, u32[]{:S(2)}) collective-permute-start(bf16[2,4,80,768]{3,1,0,2:T(4,128)(2,1)S(1)} %pad_maximum_fusion.6), channel_id=1, source_target_pairs={{0,8},{4,20},{8,0},{12,28},{16,24},{20,4},{24,16},{28,12},{1,9},{5... | collective-permute-start | bytes 2949128 | tf_op jit(solution)/shard_map/ppermute | solution.py:101
  89.6 7.4 %collective-permute-start.6 = (bf16[2,32,768]{2,1,0:T(8,128)(2,1)S(1)}, bf16[2,32,768]{2,1,0:T(8,128)(2,1)S(1)}, u32[]{:S(2)}, u32[]{:S(2)}) collective-permute-start(bf16[2,32,768]{2,1,0:T(8,128)(2,1)S(1)} %pad_maximum_fusion.16), channel_id=1, source_target_pairs={{0,2},{1,3},{2,0},{3,1},{4,6},{5,7},{6,4},{7,5},{8,10},{9,11},{10,... | collective-permute-start | bytes 294920 | tf_op jit(solution)/shard_map/ppermute | solution.py:105
  102.9 7.8 %collective-permute-start.8 = (bf16[2,4,32,768]{3,2,1,0:T(8,128)(2,1)S(1)}, bf16[2,4,32,768]{3,2,1,0:T(8,128)(2,1)S(1)}, u32[]{:S(2)}, u32[]{:S(2)}) collective-permute-start(bf16[2,4,32,768]{3,2,1,0:T(8,128)(2,1)S(1)} %pad_maximum_fusion.10), channel_id=1, source_target_pairs={{0,8},{4,20},{8,0},{12,28},{16,24},{20,4},{24,16},{28,12},{1,9},{5... | collective-permute-start | bytes 1179656 | tf_op jit(solution)/shard_map/ppermute | solution.py:101
  110.8 9.1 %collective-permute-start.9 = (bf16[2,2,4,32,768]{4,3,2,1,0:T(8,128)(2,1)S(1)}, bf16[2,2,4,32,768]{4,3,2,1,0:T(8,128)(2,1)}, u32[]{:S(2)}, u32[]{:S(2)}) collective-permute-start(bf16[2,2,4,32,768]{4,3,2,1,0:T(8,128)(2,1)S(1)} %pad_maximum_fusion.7), channel_id=1, source_target_pairs={{0,4},{4,0},{8,12},{12,8},{16,20},{20,16},{24,28},{28,24},{1,5},{5... | collective-permute-start | bytes 2359304 | tf_op jit(solution)/shard_map/ppermute | solution.py:101
  129.3 18.5 %collective-permute-start.11 = (bf16[2,112,768]{2,1,0:T(8,128)(2,1)S(1)}, bf16[2,112,768]{2,1,0:T(8,128)(2,1)S(1)}, u32[]{:S(2)}, u32[]{:S(2)}) collective-permute-start(bf16[2,112,768]{2,1,0:T(8,128)(2,1)S(1)} %pad_maximum_fusion.11), channel_id=1, source_target_pairs={{0,2},{1,3},{2,0},{3,1},{4,6},{5,7},{6,4},{7,5},{8,10},{9,11},{10,... | collective-permute-start | bytes 1032200 | tf_op jit(solution)/shard_map/ppermute | solution.py:105
  147.9 11.0 %collective-permute-start.12 = (bf16[4,112,768]{2,1,0:T(8,128)(2,1)S(1)}, bf16[4,112,768]{2,1,0:T(8,128)(2,1)S(1)}, u32[]{:S(2)}, u32[]{:S(2)}) collective-permute-start(bf16[4,112,768]{2,1,0:T(8,128)(2,1)S(1)} %bitcast.357), channel_id=1, source_target_pairs={{0,16},{4,12},{8,24},{12,4},{16,0},{20,28},{24,8},{28,20},{1,17},{... | collective-permute-start | bytes 2064392 | tf_op jit(solution)/shard_map/ppermute | solution.py:101
  160.4 18.6 %collective-permute-start.13 = (bf16[2,4,112,768]{3,2,1,0:T(8,128)(2,1)}, bf16[2,4,112,768]{3,2,1,0:T(8,128)(2,1)}, u32[]{:S(2)}, u32[]{:S(2)}) collective-permute-start(bf16[2,4,112,768]{3,2,1,0:T(8,128)(2,1)} %pad_maximum_fusion.5), channel_id=1, source_target_pairs={{0,8},{4,20},{8,0},{12,28},{16,24},{20,4},{24,16},{28,12},{1,9},{5... | collective-permute-start | bytes 4128776 | tf_op jit(solution)/shard_map/ppermute | solution.py:101
  182.7 82.1 %collective-permute-start.14 = (bf16[2,2,4,112,768]{4,3,2,1,0:T(8,128)(2,1)}, bf16[2,2,4,112,768]{4,3,2,1,0:T(8,128)(2,1)}, u32[]{:S(2)}, u32[]{:S(2)}) collective-permute-start(bf16[2,2,4,112,768]{4,3,2,1,0:T(8,128)(2,1)} %pad_maximum_fusion.2), channel_id=1, source_target_pairs={{0,4},{4,0},{8,12},{12,8},{16,20},{20,16},{24,28},{28,24},{1,5},{5... | collective-permute-start | bytes 8257544 | tf_op jit(solution)/shard_map/ppermute | solution.py:101
  304.9 257.5 %reduce-scatter.5.cloned.1.call-start = ((), (), s32[]{:S(2)}) async-start(), calls=%async_computation.3 | async-start | bytes 860160 | tf_op jit(solution)/shard_map/reduce_scatter | solution.py:313
  316.1 207.4 %collective-permute-start.20 = (bf16[2,2,4,24,768]{4,3,2,1,0:T(8,128)(2,1)}, bf16[2,2,4,24,768]{4,3,2,1,0:T(8,128)(2,1)}, u32[]{:S(2)}, u32[]{:S(2)}) collective-permute-start(bf16[2,2,4,24,768]{4,3,2,1,0:T(8,128)(2,1)} %select_convert_fusion.2), channel_id=1, source_target_pairs={{0,4},{4,0},{8,12},{12,8},{16,20},{20,16},{24,28},{28,24},{1,5},{5... | collective-permute-start | bytes 1769480 | tf_op jit(solution)/shard_map/ppermute | solution.py:101
  520.7 15.7 %collective-permute-start.15 = (bf16[2,2,4,72,768]{4,3,2,1,0:T(8,128)(2,1)S(1)}, bf16[2,2,4,72,768]{4,3,2,1,0:T(8,128)(2,1)S(1)}, u32[]{:S(2)}, u32[]{:S(2)}) collective-permute-start(bf16[2,2,4,72,768]{4,3,2,1,0:T(8,128)(2,1)S(1)} %select_convert_fusion), channel_id=1, source_target_pairs={{0,4},{4,0},{8,12},{12,8},{16,20},{20,16},{24,28},{28,24},{1,5},{5... | collective-permute-start | bytes 5308424 | tf_op jit(solution)/shard_map/ppermute | solution.py:101
  522.9 7.9 %collective-permute-start.28 = (f32[2,768]{1,0:T(2,128)S(1)}, f32[2,768]{1,0:T(2,128)S(1)}, u32[]{:S(2)}, u32[]{:S(2)}) collective-permute-start(f32[2,768]{1,0:T(2,128)S(1)} %add.168), channel_id=1, source_target_pairs={{0,1},{1,0},{2,3},{3,2},{4,5},{5,4},{6,7},{7,6},{8,9},{9,8},{10,11... | collective-permute-start | bytes 18440 | tf_op jit(solution)/shard_map/ppermute | solution.py:105
  525.0 9.1 %collective-permute-start.21 = (bf16[2,4,24,768]{3,2,1,0:T(8,128)(2,1)S(1)}, bf16[2,4,24,768]{3,2,1,0:T(8,128)(2,1)S(1)}, u32[]{:S(2)}, u32[]{:S(2)}) collective-permute-start(bf16[2,4,24,768]{3,2,1,0:T(8,128)(2,1)S(1)} %fusion.101), channel_id=1, source_target_pairs={{0,8},{4,20},{8,0},{12,28},{16,24},{20,4},{24,16},{28,12},{1,9},{5... | collective-permute-start | bytes 884744 | tf_op jit(solution)/shard_map/ppermute | solution.py:101
  530.7 23.8 %collective-permute-start.29 = (f32[2,768]{1,0:T(2,128)S(1)}, f32[2,768]{1,0:T(2,128)}, u32[]{:S(2)}, u32[]{:S(2)}) collective-permute-start(f32[2,768]{1,0:T(2,128)S(1)} %add.169), channel_id=1, source_target_pairs={{0,2},{1,3},{2,0},{3,1},{4,6},{5,7},{6,4},{7,5},{8,10},{9,11},{10,... | collective-permute-start | bytes 18440 | tf_op jit(solution)/shard_map/ppermute | solution.py:105
  534.9 20.4 %collective-permute-start.22 = (bf16[4,24,768]{2,1,0:T(8,128)(2,1)}, bf16[4,24,768]{2,1,0:T(8,128)(2,1)}, u32[]{:S(2)}, u32[]{:S(2)}) collective-permute-start(bf16[4,24,768]{2,1,0:T(8,128)(2,1)} %fusion.109), channel_id=1, source_target_pairs={{0,16},{4,12},{8,24},{12,4},{16,0},{20,28},{24,8},{28,20},{1,17},{... | collective-permute-start | bytes 442376 | tf_op jit(solution)/shard_map/ppermute | solution.py:101
  539.9 19.8 %collective-permute-start.16 = (bf16[2,4,72,768]{3,2,1,0:T(8,128)(2,1)}, bf16[2,4,72,768]{3,2,1,0:T(8,128)(2,1)}, u32[]{:S(2)}, u32[]{:S(2)}) collective-permute-start(bf16[2,4,72,768]{3,2,1,0:T(8,128)(2,1)} %fusion.96), channel_id=1, source_target_pairs={{0,8},{4,20},{8,0},{12,28},{16,24},{20,4},{24,16},{28,12},{1,9},{5... | collective-permute-start | bytes 2654216 | tf_op jit(solution)/shard_map/ppermute | solution.py:101
  540.4 48.0 %all-gather.2.cloned.1.call-start = ((), (), s32[]{:S(2)}) async-start(), calls=%async_computation.4 | async-start | bytes 1548288 | tf_op jit(solution)/shard_map/all_gather | solution.py:314
  557.8 7.2 %collective-permute-start.23 = (bf16[2,24,768]{2,1,0:T(8,128)(2,1)}, bf16[2,24,768]{2,1,0:T(8,128)(2,1)}, u32[]{:S(2)}, u32[]{:S(2)}) collective-permute-start(bf16[2,24,768]{2,1,0:T(8,128)(2,1)} %select_convert_fusion.8), channel_id=1, source_target_pairs={{0,2},{1,3},{2,0},{3,1},{4,6},{5,7},{6,4},{7,5},{8,10},{9,11},{10,... | collective-permute-start | bytes 221192 | tf_op jit(solution)/shard_map/ppermute | solution.py:105
  564.0 8.4 %collective-permute-start.17 = (bf16[4,72,768]{2,1,0:T(8,128)(2,1)S(1)}, bf16[4,72,768]{2,1,0:T(8,128)(2,1)S(1)}, u32[]{:S(2)}, u32[]{:S(2)}) collective-permute-start(bf16[4,72,768]{2,1,0:T(8,128)(2,1)S(1)} %fusion.97), channel_id=1, source_target_pairs={{0,16},{4,12},{8,24},{12,4},{16,0},{20,28},{24,8},{28,20},{1,17},{... | collective-permute-start | bytes 1327112 | tf_op jit(solution)/shard_map/ppermute | solution.py:101
  573.9 8.8 %collective-permute-start.18 = (bf16[2,72,768]{2,1,0:T(8,128)(2,1)S(1)}, bf16[2,72,768]{2,1,0:T(8,128)(2,1)S(1)}, u32[]{:S(2)}, u32[]{:S(2)}) collective-permute-start(bf16[2,72,768]{2,1,0:T(8,128)(2,1)S(1)} %select_convert_fusion.5), channel_id=1, source_target_pairs={{0,2},{1,3},{2,0},{3,1},{4,6},{5,7},{6,4},{7,5},{8,10},{9,11},{10,... | collective-permute-start | bytes 663560 | tf_op jit(solution)/shard_map/ppermute | solution.py:105
  575.0 7.9 %collective-permute-start.24 = (bf16[24,768]{1,0:T(8,128)(2,1)S(1)}, bf16[24,768]{1,0:T(8,128)(2,1)S(1)}, u32[]{:S(2)}, u32[]{:S(2)}) collective-permute-start(bf16[24,768]{1,0:T(8,128)(2,1)S(1)} %fusion.113), channel_id=1, source_target_pairs={{0,1},{1,0},{2,3},{3,2},{4,5},{5,4},{6,7},{7,6},{8,9},{9,8},{10,11... | collective-permute-start | bytes 110600 | tf_op jit(solution)/shard_map/ppermute | solution.py:105
  (68 other events, 462.8 us)
Sparse Core Ops, SparseCore 0:
  305.0 58.7 reduce-scatter.2
  540.5 20.5 reduce-scatter.4
  563.0 23.9 all-gather.1
